TPU v7x, 32 devices: a whole 2x2x4 slice. The times are simulated.
32 devices in a mesh: expert: 4 (over y, x), tensor: 2 (over core), dp: 4 (over z).
Axes of the slice: x: 2, y: 2, z: 4, core: 2. Of those that a mesh axis runs over, the one named last changes fastest.
Arguments:
- tokens: bfloat16 [2048, 3072], P(('expert', 'dp'), 'tensor'), may hold values from -6 to 6
- experts_chosen: int32 [2048, 2], P(('expert', 'dp')), may hold values from 0 to 3, all different within a row; in each aligned block of 128 rows (0 to 127, 128 to 255, ...) at most 73 rows name the same one
- route_weights: float32 [2048, 2], P(('expert', 'dp')), may hold values from 0.1 to 1
- cotangent: bfloat16 [2048, 3072], P(('expert', 'dp'), 'tensor'), may hold values from -6 to 6
- gate_weight: bfloat16 [4, 3072, 8192], P('expert', 'dp', 'tensor'), may hold values from -0.15625 to 0.15625
- up_weight: bfloat16 [4, 3072, 8192], P('expert', 'dp', 'tensor'), may hold values from -0.15625 to 0.15625
- down_weight: bfloat16 [4, 8192, 3072], P('expert', 'tensor', 'dp'), may hold values from -0.09375 to 0.09375
Outputs:
- layer_output: bfloat16 [2048, 3072], P(('expert', 'dp'), 'tensor')
- token_grad: bfloat16 [2048, 3072], P(('expert', 'dp'), 'tensor')
- route_grad: float32 [2048, 2], P(('expert', 'dp'))
Inputs may be any that keep to these rules, and one draw needn't show every extreme that they name: `experts_chosen`: each row names 2 different experts. Among the 128 rows of one index of expert+dp no expert is named more than 73 times, and in some such block one expert is named exactly 73 times.
All inputs are finite; a program needn't handle non-finite values.
Results may differ from a plain program's by a relative error of at most 0.0072.
Values may be sent and summed in bfloat16 or wider, within the bound.
No kernel may reach another device: no remote copies, remote signals or barrier semaphores. Data moves between devices by JAX's collectives and lax.ppermute only.
A program may use at most 256 MiB of HBM per device.

v0:
```python
import jax
import jax.numpy as jnp
from jax import lax
from jax.sharding import PartitionSpec as P


def slot_table(experts_chosen, num_experts, cap_rows):
    flat_ids = experts_chosen.reshape(-1)
    expert_hot = (flat_ids[:, None] == jnp.arange(num_experts, dtype=jnp.int32)[None, :]).astype(
        jnp.int32
    )
    earlier = jnp.cumsum(expert_hot, axis=0) - expert_hot
    rank_slot = jnp.sum(earlier * expert_hot, axis=1)
    target = flat_ids * cap_rows + rank_slot
    all_slots = jnp.arange(num_experts * cap_rows, dtype=jnp.int32)
    return (target[:, None] == all_slots[None, :]).astype(jnp.bfloat16)


def to_slots(slot_onehot, pair_rows, num_experts, cap_rows):
    packed = jnp.einsum("ps,pd->sd", slot_onehot, pair_rows, preferred_element_type=jnp.float32)
    return packed.astype(jnp.bfloat16).reshape(num_experts, cap_rows, pair_rows.shape[1])


def from_slots(slot_onehot, returned):
    flat_back = returned.reshape(-1, returned.shape[2])
    return jnp.dot(slot_onehot, flat_back, preferred_element_type=jnp.float32)


def as_blocks(summed, num_experts, cap_rows):
    return summed.astype(jnp.bfloat16).reshape(num_experts, cap_rows, summed.shape[1])


def local(tokens, experts_chosen, route_weights, cotangent, gate_weight, up_weight, down_weight):
    tok_rows, feat_cols = tokens.shape
    top_count = experts_chosen.shape[1]
    num_experts = lax.axis_size("expert")
    cap_rows = min(tok_rows, 9 * tok_rows * top_count // (8 * num_experts) + 1)
    slot_onehot = slot_table(experts_chosen, num_experts, cap_rows)
    pair_weights = route_weights.reshape(-1, 1)
    token_pairs = jnp.repeat(tokens, top_count, axis=0)
    grad_pairs = (
        jnp.repeat(cotangent, top_count, axis=0).astype(jnp.float32) * pair_weights
    ).astype(jnp.bfloat16)
    token_send = to_slots(slot_onehot, token_pairs, num_experts, cap_rows)
    grad_send = to_slots(slot_onehot, grad_pairs, num_experts, cap_rows)
    token_recv = lax.all_to_all(token_send, "expert", split_axis=0, concat_axis=0, tiled=True)
    token_full = lax.all_gather(token_recv, "tensor", axis=2, tiled=True)
    model_cols = token_full.shape[2]
    token_rows = token_full.reshape(-1, model_cols)
    gate_all, up_all = (
        lax.all_gather(gate_weight, "dp", axis=1, tiled=True),
        lax.all_gather(up_weight, "dp", axis=1, tiled=True),
    )
    gate_pre = jnp.dot(token_rows, gate_all[0], preferred_element_type=jnp.float32)
    up_pre = jnp.dot(token_rows, up_all[0], preferred_element_type=jnp.float32)
    hidden = (jax.nn.silu(gate_pre) * up_pre).astype(jnp.bfloat16)
    down_all = lax.all_gather(down_weight, "dp", axis=2, tiled=True)
    out_part = jnp.dot(hidden, down_all[0], preferred_element_type=jnp.float32)
    out_sum = lax.psum_scatter(
        out_part.astype(jnp.bfloat16), "tensor", scatter_dimension=1, tiled=True
    ).astype(jnp.float32)
    out_back = lax.all_to_all(
        as_blocks(out_sum, num_experts, cap_rows), "expert", split_axis=0, concat_axis=0, tiled=True
    )
    grad_recv = lax.all_to_all(grad_send, "expert", split_axis=0, concat_axis=0, tiled=True)
    grad_full = lax.all_gather(grad_recv, "tensor", axis=2, tiled=True)
    grad_rows_all = grad_full.reshape(-1, model_cols)
    contract = (((1,), (1,)), ((), ()))
    hidden_grad = lax.dot_general(
        grad_rows_all, down_all[0], contract, preferred_element_type=jnp.float32
    )
    sigmoid_gate = jax.nn.sigmoid(gate_pre)
    up_grad = (hidden_grad * jax.nn.silu(gate_pre)).astype(jnp.bfloat16)
    gate_grad = (
        hidden_grad * up_pre * sigmoid_gate * (1.0 + gate_pre * (1.0 - sigmoid_gate))
    ).astype(jnp.bfloat16)
    in_part = lax.dot_general(gate_grad, gate_all[0], contract, preferred_element_type=jnp.float32)
    in_part = in_part + lax.dot_general(
        up_grad, up_all[0], contract, preferred_element_type=jnp.float32
    )
    in_sum = lax.psum_scatter(
        in_part.astype(jnp.bfloat16), "tensor", scatter_dimension=1, tiled=True
    ).astype(jnp.float32)
    in_back = lax.all_to_all(
        as_blocks(in_sum, num_experts, cap_rows), "expert", split_axis=0, concat_axis=0, tiled=True
    )
    out_pairs = from_slots(slot_onehot, out_back).reshape(tok_rows, top_count, feat_cols)
    in_pairs = from_slots(slot_onehot, in_back).reshape(tok_rows, top_count, feat_cols)
    layer_output = jnp.sum(route_weights[:, :, None] * out_pairs, axis=1).astype(jnp.bfloat16)
    token_grad = jnp.sum(in_pairs, axis=1).astype(jnp.bfloat16)
    local_dots = jnp.sum(cotangent.astype(jnp.float32)[:, None, :] * out_pairs, axis=2)
    route_grad = lax.psum(local_dots, "tensor")
    return (layer_output, token_grad, route_grad)


def solution(mesh):
    in_specs = (
        P(("expert", "dp"), "tensor"),
        P(("expert", "dp"), None),
        P(("expert", "dp"), None),
        P(("expert", "dp"), "tensor"),
        P("expert", "dp", "tensor"),
        P("expert", "dp", "tensor"),
        P("expert", "tensor", "dp"),
    )
    out_specs = (
        P(("expert", "dp"), "tensor"),
        P(("expert", "dp"), "tensor"),
        P(("expert", "dp"), None),
    )
    return jax.shard_map(local, mesh=mesh, in_specs=in_specs, out_specs=out_specs, check_vma=False)
```

profile of v0, /device:TPU:0, one launch (start us, length us, event | category | flops | bytes accessed | tf_op | source)
XLA Modules:
  0.0 1455.3 jit_solution(10602917999644850191)
XLA Ops:
  7.2 0.8 copy.21
  8.3 1.4 broadcast_in_dim.4
  10.1 1.2 reduce-window.6
  12.5 18.7 %all_to_all.20 = bf16[4,73,1536]{2,1,0:T(8,128)(2,1)} all-to-all(bf16[4,73,1536]{2,1,0:T(8,128)(2,1)S(1)} %reshape.107), channel_id=1, replica_groups=mesh['expert'=4,'tensor'=2,'dp'=4] {'expert'}, dimensions={0} | all-to-all | bytes 1794048 | tf_op jit(solution)/shard_map/all_to_all | solution.py:46
  31.7 1.1 convert_element_type.57
  33.0 0.5 convolution_convert_fusion
  33.8 15.7 %all_to_all.21 = bf16[4,73,1536]{2,1,0:T(8,128)(2,1)} all-to-all(bf16[4,73,1536]{2,1,0:T(8,128)(2,1)S(1)} %reshape.111), channel_id=1, replica_groups=mesh['expert'=4,'tensor'=2,'dp'=4] {'expert'}, dimensions={0} | all-to-all | bytes 1794048 | tf_op jit(solution)/shard_map/all_to_all | solution.py:65
  49.6 0.7 all-gather.10.cloned.1.call-update
  50.9 0.5 all-gather.12.cloned.1.call-update
  51.7 2.0 reshape.108
  53.7 5.9 all-gather.14.cloned.1.call-done
  59.6 3.3 reshape.112
  62.9 424.7 %all-gather.10.cloned.1.call-done = bf16[1,3072,4096]{2,1,0:T(8,128)(2,1)} async-done(((bf16[1,768,4096]{2,1,0:T(8,128)(2,1)}), bf16[1,3072,4096]{2,1,0:T(8,128)(2,1)}) %all-gather.10.cloned.1.call-update) | async-done | bytes 25165840 | tf_op jit(solution)/shard_map/all_gather | solution.py:52
  487.6 16.4 %fusion.6 = f32[292,4096]{1,0:T(8,128)} fusion(bf16[292,3072]{1,0:T(8,128)(2,1)S(1)} %reshape.108, bf16[1,3072,4096]{2,1,0:T(8,128)(2,1)} %all-gather.10.cloned.1.call-done), kind=kOutput, calls=%fused_computation.6 | convolution fusion | flops 7348420608 | bytes 31744000 | tf_op jit(solution)/shard_map/dot_general | solution.py:55
  504.0 408.4 %all-gather.8.cloned.1.call-done = bf16[1,3072,4096]{2,1,0:T(8,128)(2,1)} async-done(((bf16[1,768,4096]{2,1,0:T(8,128)(2,1)}), bf16[1,3072,4096]{2,1,0:T(8,128)(2,1)}) %all-gather.8.cloned.1.call-update) | async-done | bytes 25165840 | tf_op jit(solution)/shard_map/all_gather | solution.py:51
  912.4 16.3 %fusion.10 = f32[292,4096]{1,0:T(8,128)} fusion(bf16[292,3072]{1,0:T(8,128)(2,1)S(1)} %reshape.108, bf16[1,3072,4096]{2,1,0:T(8,128)(2,1)} %all-gather.8.cloned.1.call-done), kind=kOutput, calls=%fused_computation.10 | convolution fusion | flops 7348420608 | bytes 31744000 | tf_op jit(solution)/shard_map/dot_general | solution.py:54
  928.8 408.5 %all-gather.12.cloned.1.call-done = bf16[1,4096,3072]{2,1,0:T(8,128)(2,1)} async-done(((bf16[1,4096,768]{2,1,0:T(8,128)(2,1)}), bf16[1,4096,3072]{2,1,0:T(8,128)(2,1)}) %all-gather.12.cloned.1.call-update) | async-done | bytes 25165840 | tf_op jit(solution)/shard_map/all_gather | solution.py:57
  1337.3 14.5 fusion
  1351.7 16.7 %fusion.4 = f32[292,3072]{1,0:T(8,128)} fusion(bf16[1,3072,4096]{2,1,0:T(8,128)(2,1)} %all-gather.10.cloned.1.call-done, f32[292,4096]{1,0:T(8,128)} %fusion, f32[292,4096]{1,0:T(8,128)} %fusion.10), kind=kOutput, calls=%fused_computation.4 | convolution fusion | flops 7355596800 | bytes 38322176 | tf_op jit(solution)/shard_map/dot_general | solution.py:78
  1368.5 21.3 %fusion.16 = bf16[292,3072]{1,0:T(8,128)(2,1)} fusion(f32[292,3072]{1,0:T(8,128)} %fusion.4, bf16[1,3072,4096]{2,1,0:T(8,128)(2,1)} %all-gather.8.cloned.1.call-done, f32[292,4096]{1,0:T(8,128)} %fusion.10, f32[292,4096]{1,0:T(8,128)} %fusion, f32[292,4096]{1,0:T(8,128)} %fusion.6), kind=kOutput, calls=%fused_computation.18 | convolution fusion | flops 7362174976 | bytes 44900352 | tf_op jit(solution)/shard_map/dot_general | solution.py:77
  1389.9 17.2 %fusion.19 = bf16[292,3072]{1,0:T(8,128)(2,1)} fusion(bf16[1,4096,3072]{2,1,0:T(8,128)(2,1)} %all-gather.12.cloned.1.call-done, f32[292,4096]{1,0:T(8,128)} %fusion.6, f32[292,4096]{1,0:T(8,128)} %fusion.10), kind=kOutput, calls=%fused_computation.19 | convolution fusion | flops 7356493824 | bytes 36528128 | tf_op jit(solution)/shard_map/dot_general | solution.py:58
  1407.1 2.4 reshape.113
  1409.5 3.6 all-to-all-start.3
  1413.2 1.5 reduce-scatter.3.cloned.1.call-done
  1414.7 2.4 reshape.109
  1417.1 9.3 all-to-all-done.3
  1426.5 3.5 all-to-all-start.1
  1430.0 1.0 convert_element_type.56
  1431.5 1.4 convolution_reduce_fusion
  1432.8 9.6 all-to-all-done.1
  1442.7 2.7 multiply_reduce_fusion
  1445.4 3.0 psum.7
  (43 shorter events, 4.5 us)
Async XLA Ops:
  7.2 24.1 %copy-start = (bf16[128,1536]{1,0:T(8,128)(2,1)S(1)}, bf16[128,1536]{1,0:T(8,128)(2,1)}, u32[]{:S(2)}) copy-start(bf16[128,1536]{1,0:T(8,128)(2,1)} %param.10) | copy-start | bytes 1179652
  7.2 44.5 %all-gather.6.cloned.1.call-start = ((), (), s32[]{:S(2)}) async-start(), calls=%async_computation.6 | async-start | bytes 2949120 | tf_op jit(solution)/shard_map/all_gather | solution.py:47
  12.2 20.5 %copy-start.2 = (f32[128,2]{0,1:T(2,128)S(1)}, f32[128,2]{0,1:T(2,128)}, u32[]{:S(2)}) copy-start(f32[128,2]{0,1:T(2,128)} %param.9) | copy-start | bytes 3076
  31.2 28.4 %all-gather.14.cloned.1.call-start = ((), (), s32[]{:S(2)}) async-start(), calls=%async_computation.11 | async-start | bytes 2949120 | tf_op jit(solution)/shard_map/all_gather | solution.py:66
  49.5 438.1 %all-gather.10.cloned.1.call-start = ((), (), s32[]{:S(2)}) async-start(), calls=%async_computation.8 | async-start | bytes 31457280 | tf_op jit(solution)/shard_map/all_gather | solution.py:52
  50.3 862.2 %all-gather.8.cloned.1.call-start = ((), (), s32[]{:S(2)}) async-start(), calls=%async_computation.7 | async-start | bytes 31457280 | tf_op jit(solution)/shard_map/all_gather | solution.py:51
  50.9 1286.4 %all-gather.12.cloned.1.call-start = ((), (), s32[]{:S(2)}) async-start(), calls=%async_computation.9 | async-start | bytes 31457280 | tf_op jit(solution)/shard_map/all_gather | solution.py:57
  51.5 1355.7 %reduce-scatter.5.cloned.1.call-start = ((), (), s32[]{:S(2)}) async-start(), calls=%async_computation.12 | async-start | bytes 2727936 | tf_op jit(solution)/shard_map/reduce_scatter | solution.py:81
  1389.8 24.9 %reduce-scatter.3.cloned.1.call-start = ((), (), s32[]{:S(2)}) async-start(), calls=%async_computation.10 | async-start | bytes 2727936 | tf_op jit(solution)/shard_map/reduce_scatter | solution.py:59
  1407.1 24.1 %copy-start.1 = (s32[128,2]{0,1:T(2,128)S(1)}, s32[128,2]{0,1:T(2,128)}, u32[]{:S(2)}) copy-start(s32[128,2]{0,1:T(2,128)} %param.8) | copy-start | bytes 3076
  1409.5 16.9 %all-to-all-start.3 = ((bf16[4,73,1536]{2,1,0:T(8,128)(2,1)}), bf16[4,73,1536]{2,1,0:T(8,128)(2,1)S(1)}, u32[]{:S(2)}, u32[]{:S(2)}) async-start(bf16[4,73,1536]{2,1,0:T(8,128)(2,1)} %reshape.113), calls=%async_computation.5 | async-start | bytes 1966080 | tf_op jit(solution)/shard_map/all_to_all | solution.py:84
  1426.5 16.0 %all-to-all-start.1 = ((bf16[4,73,1536]{2,1,0:T(8,128)(2,1)}), bf16[4,73,1536]{2,1,0:T(8,128)(2,1)S(1)}, u32[]{:S(2)}, u32[]{:S(2)}) async-start(bf16[4,73,1536]{2,1,0:T(8,128)(2,1)} %reshape.109), calls=%async_computation.2 | async-start | bytes 1966080 | tf_op jit(solution)/shard_map/all_to_all | solution.py:62
Sparse Core Ops, SparseCore 0:
  31.3 9.9 all-gather.5
  49.7 9.9 all-gather.13
  61.2 426.3 all-gather.9
  489.0 423.3 all-gather.7
  913.9 423.3 all-gather.11
  1389.9 7.5 reduce-scatter.4
  1407.2 7.4 reduce-scatter.2
where the time goes:
time: 1460 us
  waiting for transfers between devices  1270 us (87%)
  matrix products  108 us (7%)
  blocking collectives  37.4 us (3%)
  local copies, waits for them, and re-layouts  16.2 us (1%)
    all_gather x1, waiting for transfers between devices, local(): lax.all_gather(up_weight, 'dp', axis=1, tiled=True)  425 us
    all_gather x1, waiting for transfers between devices, local(): down_all = lax.all_gather(down_weight, 'dp', axis=2, tiled=True)  408 us
    all_gather x1, waiting for transfers between devices, local(): lax.all_gather(gate_weight, 'dp', axis=1, tiled=True)  408 us
  transfers between devices with their start and end apart: 9, of which 7 were waited for; matrix products, arithmetic and copies ran while one was open for 4% of the time, Pallas kernels for 0%

commit v1 on v0

--- a/solution.py
+++ b/solution.py
@@ -2,6 +2,23 @@
 import jax.numpy as jnp
 from jax import lax
 from jax.sharding import PartitionSpec as P
+
+
+def joined_along(parts, dim):
+    parts = jnp.moveaxis(parts, 0, dim)
+    lengths = parts.shape
+    return parts.reshape(*lengths[:dim], lengths[dim] * lengths[dim + 1], *lengths[dim + 2 :])
+
+
+def gather_around(shard, axis, dim):
+    count = lax.axis_size(axis)
+    right = [(i, (i + 1) % count) for i in range(count)]
+    parts = [shard]
+    while len(parts) < count:
+        parts.append(lax.ppermute(parts[-1], axis, right))
+    here = lax.axis_index(axis)
+    parts = jnp.stack(parts)[(here - jnp.arange(count)) % count]
+    return joined_along(parts, dim)
 
 
 def slot_table(experts_chosen, num_experts, cap_rows):
@@ -48,7 +65,7 @@
     model_cols = token_full.shape[2]
     token_rows = token_full.reshape(-1, model_cols)
     gate_all, up_all = (
-        lax.all_gather(gate_weight, "dp", axis=1, tiled=True),
+        gather_around(gate_weight, "dp", 1),
         lax.all_gather(up_weight, "dp", axis=1, tiled=True),
     )
     gate_pre = jnp.dot(token_rows, gate_all[0], preferred_element_type=jnp.float32)

time: 1460 us -> 1390 us (0.952)
  waiting for transfers between devices: 1270 us -> 949 us
  starting transfers between devices: 7.58 us -> 177 us
  local copies, waits for them, and re-layouts: 16.2 us -> 64 us
  other arithmetic: 2.35 us -> 40.8 us
    ppermute x0 -> x3, waiting for transfers between devices: none -> 754 us  [gather_around(): parts.append(lax.ppermute(parts[-1], axis, right))]
    all_gather x1, waiting for transfers between devices: 425 us -> 0.01 us  [local(): lax.all_gather(up_weight, 'dp', axis=1, tiled=True)]
    all_gather x1 -> x0, waiting for transfers between devices: 408 us -> none  [local(): lax.all_gather(gate_weight, 'dp', axis=1, tiled=True)]
    all_gather x1, waiting for transfers between devices: 408 us -> 173 us  [local(): down_all = lax.all_gather(down_weight, 'dp', axis=2, tiled=True)]
    ppermute x0 -> x3, starting transfers between devices: none -> 169 us  [gather_around(): parts.append(lax.ppermute(parts[-1], axis, right))]
    gather x0 -> x5, local copies, waits for them, and re-layouts: none -> 44.6 us  [gather_around(): parts = jnp.stack(parts)[(here - jnp.arange(count)) % count]]
    another operation x2 -> x3, other arithmetic: 1.26 us -> 22.1 us  [the longest x1 20.8 us: gather_around(): parts = jnp.stack(parts)[(here - jnp.arange(count)) % count]]
    unnamed x1 -> x2, other arithmetic: 0.07 us -> 17.7 us
  transfers between devices with their start and end apart: 9 -> 11, of which waited for: 7 -> 7; matrix products, arithmetic and copies ran while one was open for 4% -> 10% of each run, Pallas kernels for 0% -> 0%
where the time goes in v1:
time: 1390 us
  waiting for transfers between devices  949 us (68%)
  starting transfers between devices  177 us (13%)
  matrix products  104 us (7%)
  local copies, waits for them, and re-layouts  64 us (5%)
  other arithmetic  40.8 us (3%)
  blocking collectives  37.3 us (3%)
  between operations  14.3 us (1%)
    ppermute x3, waiting for transfers between devices, gather_around(): parts.append(lax.ppermute(parts[-1], axis, right))  754 us
    all_gather x1, waiting for transfers between devices, local(): down_all = lax.all_gather(down_weight, 'dp', axis=2, tiled=True)  173 us
    ppermute x3, starting transfers between devices, gather_around(): parts.append(lax.ppermute(parts[-1], axis, right))  169 us
    gather x5, local copies, waits for them, and re-layouts, gather_around(): parts = jnp.stack(parts)[(here - jnp.arange(count)) % count]  44.6 us
  transfers between devices with their start and end apart: 11, of which 7 were waited for; matrix products, arithmetic and copies ran while one was open for 10% of the time, Pallas kernels for 0%

profile of v1, /device:TPU:0, one launch (start us, length us, event | category | flops | bytes accessed | tf_op | source)
XLA Modules:
  0.0 1386.0 jit_solution(8597672696583736749)
XLA Ops:
  13.1 18.7 %all_to_all.20 = bf16[4,73,1536]{2,1,0:T(8,128)(2,1)} all-to-all(bf16[4,73,1536]{2,1,0:T(8,128)(2,1)S(1)} %reshape.156), channel_id=1, replica_groups=mesh['expert'=4,'tensor'=2,'dp'=4] {'expert'}, dimensions={0} | all-to-all | bytes 1794048 | tf_op jit(solution)/shard_map/all_to_all | solution.py:63
  34.4 15.7 %all_to_all.21 = bf16[4,73,1536]{2,1,0:T(8,128)(2,1)} all-to-all(bf16[4,73,1536]{2,1,0:T(8,128)(2,1)S(1)} %reshape.160), channel_id=1, replica_groups=mesh['expert'=4,'tensor'=2,'dp'=4] {'expert'}, dimensions={0} | all-to-all | bytes 1794048 | tf_op jit(solution)/shard_map/all_to_all | solution.py:82
  53.1 244.2 %collective-permute-done = bf16[1,768,4096]{2,1,0:T(8,128)(2,1)S(1)} collective-permute-done((bf16[1,768,4096]{2,1,0:T(8,128)(2,1)}, bf16[1,768,4096]{2,1,0:T(8,128)(2,1)S(1)}, u32[]{:S(2)}, u32[]{:S(2)}) %collective-permute-start) | collective-permute-done | bytes 6291488 | tf_op jit(solution)/shard_map/ppermute | solution.py:18
  297.3 2.6 copy-done
  299.9 120.0 %collective-permute-start.1 = (bf16[1,768,4096]{2,1,0:T(8,128)(2,1)S(1)}, bf16[1,768,4096]{2,1,0:T(8,128)(2,1)}, u32[]{:S(2)}, u32[]{:S(2)}) collective-permute-start(bf16[1,768,4096]{2,1,0:T(8,128)(2,1)S(1)} %collective-permute-done), channel_id=1, source_target_pairs={{0,1},{1,2},{2,3},{3,0},{4,5},{5,6},{6,7},{7,4},{8,9},{9,10},{10,1... | collective-permute-start | bytes 18874376 | tf_op jit(solution)/shard_map/ppermute | solution.py:18
  419.9 260.2 %collective-permute-done.1 = bf16[1,768,4096]{2,1,0:T(8,128)(2,1)} collective-permute-done((bf16[1,768,4096]{2,1,0:T(8,128)(2,1)S(1)}, bf16[1,768,4096]{2,1,0:T(8,128)(2,1)}, u32[]{:S(2)}, u32[]{:S(2)}) %collective-permute-start.1) | collective-permute-done | bytes 6291488 | tf_op jit(solution)/shard_map/ppermute | solution.py:18
  680.1 47.7 %collective-permute-start.2 = (bf16[1,768,4096]{2,1,0:T(8,128)(2,1)}, bf16[1,768,4096]{2,1,0:T(8,128)(2,1)}, u32[]{:S(2)}, u32[]{:S(2)}) collective-permute-start(bf16[1,768,4096]{2,1,0:T(8,128)(2,1)} %collective-permute-done.1), channel_id=1, source_target_pairs={{0,1},{1,2},{2,3},{3,0},{4,5},{5,6},{6,7},{7,4},{8,9},{9,10},{10,1... | collective-permute-start | bytes 18874376 | tf_op jit(solution)/shard_map/ppermute | solution.py:18
  727.9 2.0 reshape.157
  729.9 3.3 reshape.161
  733.2 249.9 %collective-permute-done.2 = bf16[1,768,4096]{2,1,0:T(8,128)(2,1)} collective-permute-done((bf16[1,768,4096]{2,1,0:T(8,128)(2,1)}, bf16[1,768,4096]{2,1,0:T(8,128)(2,1)}, u32[]{:S(2)}, u32[]{:S(2)}) %collective-permute-start.2) | collective-permute-done | bytes 6291488 | tf_op jit(solution)/shard_map/ppermute | solution.py:18
  983.1 20.8 %pad_maximum_fusion = bf16[4,1,768,4096]{3,2,1,0:T(8,128)(2,1)} fusion(bf16[1,1,768,4096]{3,2,1,0:T(8,128)(2,1)} %bitcast.6, bf16[1,1,768,4096]{3,2,1,0:T(8,128)(2,1)} %bitcast.5, bf16[1,1,768,4096]{3,2,1,0:T(8,128)(2,1)} %bitcast.75, bf16[1,1,768,4096]{3,2,1,0:T(8,128)(2,1)} %bitcast.74), kind=kLoop, calls=%fused_computation.4 | loop fusion | flops 37748736 | bytes 50331648 | tf_op jit(solution)/shard_map/stack | solution.py:20
  1003.9 19.1 %slice_bitcast_fusion.3 = (bf16[4,768,1024]{2,1,0:T(8,128)(2,1)}, bf16[4,768,1024]{2,1,0:T(8,128)(2,1)}, bf16[4,768,1024]{2,1,0:T(8,128)(2,1)}, bf16[4,768,1024]{2,1,0:T(8,128)(2,1)}) fusion(bf16[4,1,768,4096]{3,2,1,0:T(8,128)(2,1)} %pad_maximum_fusion), kind=kLoop, calls=%fused_computation.17 | loop fusion | bytes 50331648 | tf_op jit(solution)/shard_map/gather | solution.py:20
  1023.0 6.4 gather_fusion.1
  1029.4 6.4 gather_fusion.2
  1035.8 6.4 gather_fusion.3
  1042.2 6.3 gather_fusion
  1048.5 17.7 %pad_maximum_fusion.1 = bf16[4,1,768,4096]{3,2,0,1:T(8,128)(2,1)} fusion(bf16[4,1,768,1024]{3,2,0,1:T(8,128)(2,1)} %bitcast.72, bf16[4,1,768,1024]{3,2,0,1:T(8,128)(2,1)} %bitcast.71, bf16[4,1,768,1024]{3,2,0,1:T(8,128)(2,1)} %bitcast.70, bf16[4,1,768,1024]{3,2,0,1:T(8,128)(2,1)} %bitcast.73), kind=kLoop, calls=%fused_computation.5 | loop fusion | flops 100663296 | bytes 50331648
  1066.2 14.4 %fusion.39 = f32[292,4096]{1,0:T(8,128)} fusion(bf16[292,3072]{1,0:T(8,128)(2,1)S(1)} %reshape.157, bf16[3072,4096]{1,0:T(8,128)(2,1)} %bitcast.68), kind=kOutput, calls=%fused_computation.62 | convolution fusion | flops 7348420608 | bytes 31744000 | tf_op jit(solution)/shard_map/dot_general | solution.py:71
  1080.6 14.5 %fusion.6 = f32[292,4096]{1,0:T(8,128)} fusion(bf16[292,3072]{1,0:T(8,128)(2,1)S(1)} %reshape.157, bf16[1,3072,4096]{2,1,0:T(8,128)(2,1)} %all-gather.7.cloned.1.call-done), kind=kOutput, calls=%fused_computation.12 | convolution fusion | flops 7348420608 | bytes 31744000 | tf_op jit(solution)/shard_map/dot_general | solution.py:72
  1095.1 172.6 %all-gather.9.cloned.1.call-done = bf16[1,4096,3072]{2,1,0:T(8,128)(2,1)} async-done(((bf16[1,4096,768]{2,1,0:T(8,128)(2,1)}), bf16[1,4096,3072]{2,1,0:T(8,128)(2,1)}) %all-gather.9.cloned.1.call-update) | async-done | bytes 25165840 | tf_op jit(solution)/shard_map/all_gather | solution.py:74
  1267.8 14.5 %fusion = f32[292,4096]{1,0:T(8,128)} fusion(bf16[292,3072]{1,0:T(8,128)(2,1)} %reshape.161, bf16[1,4096,3072]{2,1,0:T(8,128)(2,1)} %all-gather.9.cloned.1.call-done), kind=kOutput, calls=%fused_computation.6 | convolution fusion | flops 7348420608 | bytes 31744000 | tf_op jit(solution)/shard_map/dot_general | solution.py:86
  1282.3 21.1 %fusion.18 = f32[292,3072]{1,0:T(8,128)} fusion(bf16[3072,4096]{1,0:T(8,128)(2,1)} %bitcast.69, f32[292,4096]{1,0:T(8,128)} %fusion.39, f32[292,4096]{1,0:T(8,128)} %fusion, f32[292,4096]{1,0:T(8,128)} %fusion.6), kind=kOutput, calls=%fused_computation.28 | convolution fusion | flops 7360380928 | bytes 43106304 | tf_op jit(solution)/shard_map/dot_general | solution.py:94
  1303.4 17.0 %fusion.12 = bf16[292,3072]{1,0:T(8,128)(2,1)} fusion(f32[292,3072]{1,0:T(8,128)} %fusion.18, bf16[1,3072,4096]{2,1,0:T(8,128)(2,1)} %all-gather.7.cloned.1.call-done, f32[292,4096]{1,0:T(8,128)} %fusion, f32[292,4096]{1,0:T(8,128)} %fusion.39), kind=kOutput, calls=%fused_computation.24 | convolution fusion | flops 7357390848 | bytes 40116224 | tf_op jit(solution)/shard_map/dot_general | solution.py:95
  1320.4 17.2 %fusion.15 = bf16[292,3072]{1,0:T(8,128)(2,1)} fusion(bf16[1,4096,3072]{2,1,0:T(8,128)(2,1)} %all-gather.9.cloned.1.call-done, f32[292,4096]{1,0:T(8,128)} %fusion.6, f32[292,4096]{1,0:T(8,128)} %fusion.39), kind=kOutput, calls=%fused_computation.25 | convolution fusion | flops 7356493824 | bytes 36528128 | tf_op jit(solution)/shard_map/dot_general | solution.py:75
  1337.7 2.4 reshape.162
  1340.2 3.5 all-to-all-start.3
  1344.3 2.4 reshape.158
  1346.7 10.4 all-to-all-done.3
  1357.1 3.5 all-to-all-start.1
  1363.4 9.7 all-to-all-done.1
  1373.4 2.7 multiply_reduce_fusion
  1376.1 3.0 psum.7
  (65 shorter events, 15.2 us)
Async XLA Ops:
  7.2 24.7 %copy-start.1 = (bf16[128,1536]{1,0:T(8,128)(2,1)S(1)}, bf16[128,1536]{1,0:T(8,128)(2,1)}, u32[]{:S(2)}) copy-start(bf16[128,1536]{1,0:T(8,128)(2,1)} %param.10) | copy-start | bytes 1179652
  7.2 720.7 %all-gather.5.cloned.1.call-start = ((), (), s32[]{:S(2)}) async-start(), calls=%async_computation.6 | async-start | bytes 2949120 | tf_op jit(solution)/shard_map/all_gather | solution.py:64
  10.0 0.6 copy-start.3
  12.8 20.5 %copy-start.6 = (f32[128,2]{0,1:T(2,128)S(1)}, f32[128,2]{0,1:T(2,128)}, u32[]{:S(2)}) copy-start(f32[128,2]{0,1:T(2,128)} %param.9) | copy-start | bytes 3076
  31.8 698.2 %all-gather.11.cloned.1.call-start = ((), (), s32[]{:S(2)}) async-start(), calls=%async_computation.10 | async-start | bytes 2949120 | tf_op jit(solution)/shard_map/all_gather | solution.py:83
  50.1 1030.6 %all-gather.7.cloned.1.call-start = ((), (), s32[]{:S(2)}) async-start(), calls=%async_computation.7 | async-start | bytes 31457280 | tf_op jit(solution)/shard_map/all_gather | solution.py:69
  50.8 1216.9 %all-gather.9.cloned.1.call-start = ((), (), s32[]{:S(2)}) async-start(), calls=%async_computation.8 | async-start | bytes 31457280 | tf_op jit(solution)/shard_map/all_gather | solution.py:74
  51.4 1286.3 %reduce-scatter.5.cloned.1.call-start = ((), (), s32[]{:S(2)}) async-start(), calls=%async_computation.11 | async-start | bytes 2727936 | tf_op jit(solution)/shard_map/reduce_scatter | solution.py:98
  51.4 245.9 %collective-permute-start = (bf16[1,768,4096]{2,1,0:T(8,128)(2,1)}, bf16[1,768,4096]{2,1,0:T(8,128)(2,1)S(1)}, u32[]{:S(2)}, u32[]{:S(2)}) collective-permute-start(bf16[1,768,4096]{2,1,0:T(8,128)(2,1)} %param.11), channel_id=1, source_target_pairs={{0,1},{1,2},{2,3},{3,0},{4,5},{5,6},{6,7},{7,4},{8,9},{9,10},{10,1... | collective-permute-start | bytes 18874376 | tf_op jit(solution)/shard_map/ppermute | solution.py:18
  297.3 2.6 copy-start
  299.9 380.2 %collective-permute-start.1 = (bf16[1,768,4096]{2,1,0:T(8,128)(2,1)S(1)}, bf16[1,768,4096]{2,1,0:T(8,128)(2,1)}, u32[]{:S(2)}, u32[]{:S(2)}) collective-permute-start(bf16[1,768,4096]{2,1,0:T(8,128)(2,1)S(1)} %collective-permute-done), channel_id=1, source_target_pairs={{0,1},{1,2},{2,3},{3,0},{4,5},{5,6},{6,7},{7,4},{8,9},{9,10},{10,1... | collective-permute-start | bytes 18874376 | tf_op jit(solution)/shard_map/ppermute | solution.py:18
  680.1 303.1 %collective-permute-start.2 = (bf16[1,768,4096]{2,1,0:T(8,128)(2,1)}, bf16[1,768,4096]{2,1,0:T(8,128)(2,1)}, u32[]{:S(2)}, u32[]{:S(2)}) collective-permute-start(bf16[1,768,4096]{2,1,0:T(8,128)(2,1)} %collective-permute-done.1), channel_id=1, source_target_pairs={{0,1},{1,2},{2,3},{3,0},{4,5},{5,6},{6,7},{7,4},{8,9},{9,10},{10,1... | collective-permute-start | bytes 18874376 | tf_op jit(solution)/shard_map/ppermute | solution.py:18
  1320.4 23.9 %reduce-scatter.3.cloned.1.call-start = ((), (), s32[]{:S(2)}) async-start(), calls=%async_computation.9 | async-start | bytes 2727936 | tf_op jit(solution)/shard_map/reduce_scatter | solution.py:76
  1337.7 22.9 %copy-start.4 = (s32[256]{0:T(256)S(1)}, s32[256]{0:T(256)}, u32[]{:S(2)}) copy-start(s32[256]{0:T(256)} %copy-done.3) | copy-start | bytes 3076
  1337.7 23.1 %copy-start.2 = (bf16[128,1536]{1,0:T(8,128)(2,1)S(1)}, bf16[128,1536]{1,0:T(8,128)(2,1)}, u32[]{:S(2)}) copy-start(bf16[128,1536]{1,0:T(8,128)(2,1)} %param.10) | copy-start | bytes 1179652
  1337.7 24.1 %copy-start.5 = (s32[128,2]{0,1:T(2,128)S(1)}, s32[128,2]{0,1:T(2,128)}, u32[]{:S(2)}) copy-start(s32[128,2]{0,1:T(2,128)} %param.8) | copy-start | bytes 3076
  1340.2 16.9 %all-to-all-start.3 = ((bf16[4,73,1536]{2,1,0:T(8,128)(2,1)}), bf16[4,73,1536]{2,1,0:T(8,128)(2,1)S(1)}, u32[]{:S(2)}, u32[]{:S(2)}) async-start(bf16[4,73,1536]{2,1,0:T(8,128)(2,1)} %reshape.162), calls=%async_computation.5 | async-start | bytes 1966080 | tf_op jit(solution)/shard_map/all_to_all | solution.py:101
  1343.7 29.7 %copy-start.7 = (f32[128,2]{0,1:T(2,128)S(1)}, f32[128,2]{0,1:T(2,128)}, u32[]{:S(2)}) copy-start(f32[128,2]{0,1:T(2,128)} %param.9) | copy-start | bytes 3076
  1357.1 16.1 %all-to-all-start.1 = ((bf16[4,73,1536]{2,1,0:T(8,128)(2,1)}), bf16[4,73,1536]{2,1,0:T(8,128)(2,1)S(1)}, u32[]{:S(2)}, u32[]{:S(2)}) async-start(bf16[4,73,1536]{2,1,0:T(8,128)(2,1)} %reshape.158), calls=%async_computation.2 | async-start | bytes 1966080 | tf_op jit(solution)/shard_map/all_to_all | solution.py:79
Sparse Core Ops, SparseCore 0:
  31.9 9.9 all-gather.4
  50.2 9.9 all-gather.10
  61.7 667.5 all-gather.6
  730.8 536.9 all-gather.8
  1320.5 6.7 reduce-scatter.4
  1337.8 6.4 reduce-scatter.2
